TPU v7x, 32 devices: a whole 2x2x4 slice. The times are simulated.
32 devices in a mesh: dp: 8 (over z, y), mp: 4 (over x, core).
Axes of the slice: x: 2, y: 2, z: 4, core: 2. Of those that a mesh axis runs over, the one named last changes fastest.
Arguments:
- sentence_entry_words: bfloat16 [16384, 768], P(('dp', 'mp')), may hold values from -6 to 6
- sentence_present_marks: int32 [1024], P(('dp', 'mp')), may hold values 0 or 1
- picture_present_marks: int32 [1024], P(('dp', 'mp')), may hold values 0 or 1
- matched_picture_positions: int32 [1024], replicated, may hold values from 0 to 1023, each once
- stored_picture_patches: bfloat16 [51200, 768], P(('dp', 'mp')), may hold values from -6 to 6
- log_logit_multiplier: float32 [1], replicated, may hold values from 3.6 to 4.3
- leading_standardizer_stretch: float32 [768], replicated, may hold values from 0.5 to 1.5
- leading_standardizer_shift: float32 [768], replicated, may hold values from -1 to 1
- lookup_coefficients: bfloat16 [768, 768], P(None, 'mp'), may hold values from -0.21875 to 0.21875
- lookup_offset: float32 [768], P('mp'), may hold values from -1 to 1
- address_coefficients: bfloat16 [768, 768], P(None, 'mp'), may hold values from -0.21875 to 0.21875
- content_coefficients: bfloat16 [768, 768], P(None, 'mp'), may hold values from -0.21875 to 0.21875
- content_offset: float32 [768], P('mp'), may hold values from -1 to 1
- mixer_exit_coefficients: bfloat16 [768, 768], P('mp'), may hold values from -0.625 to 0.625
- mixer_exit_offset: float32 [768], replicated, may hold values from -1 to 1
- trailing_standardizer_stretch: float32 [768], replicated, may hold values from 0.5 to 1.5
- trailing_standardizer_shift: float32 [768], replicated, may hold values from -1 to 1
- perceptron_entry_coefficients: bfloat16 [768, 3072], P(None, 'mp'), may hold values from -0.21875 to 0.21875
- perceptron_inner_offset: float32 [3072], P('mp'), may hold values from -1 to 1
- perceptron_exit_coefficients: bfloat16 [3072, 768], P('mp'), may hold values from -0.109375 to 0.109375
- perceptron_exit_offset: float32 [768], replicated, may hold values from -1 to 1
- picture_lookup_coefficients: bfloat16 [768, 768], replicated, may hold values from -0.21875 to 0.21875
- picture_address_coefficients: bfloat16 [768, 768], replicated, may hold values from -0.21875 to 0.21875
- picture_content_coefficients: bfloat16 [768, 768], replicated, may hold values from -0.21875 to 0.21875
- picture_mixer_exit: bfloat16 [768, 768], replicated, may hold values from -0.625 to 0.625
- picture_perceptron_entry: bfloat16 [768, 3072], replicated, may hold values from -0.21875 to 0.21875
- picture_perceptron_exit: bfloat16 [3072, 768], replicated, may hold values from -0.109375 to 0.109375
Outputs:
- loss: float32 [1], replicated
- text_out: bfloat16 [16384, 768], P(('dp', 'mp'))
- text_in_grad: float32 [16384, 768], P(('dp', 'mp'))
- temperature_grad: float32 [1], replicated
- ln1_gain_grad: float32 [768], replicated
- ln1_bias_grad: float32 [768], replicated
- w_query_grad: float32 [768, 768], P(None, 'mp')
- query_bias_grad: float32 [768], P('mp')
- w_key_grad: float32 [768, 768], P(None, 'mp')
- w_value_grad: float32 [768, 768], P(None, 'mp')
- value_bias_grad: float32 [768], P('mp')
- w_attn_out_grad: float32 [768, 768], P('mp')
- attn_out_bias_grad: float32 [768], replicated
- ln2_gain_grad: float32 [768], replicated
- ln2_bias_grad: float32 [768], replicated
- w_hidden_grad: float32 [768, 3072], P(None, 'mp')
- hidden_bias_grad: float32 [3072], P('mp')
- w_proj_grad: float32 [3072, 768], P('mp')
- proj_bias_grad: float32 [768], replicated
Inputs may be any that keep to these rules, and one draw needn't show every extreme that they name: `matched_picture_positions`: each index appears exactly once.
All inputs are finite; a program needn't handle non-finite values. No bound on the sum of `sentence_present_marks` or of `picture_present_marks` on one device may be relied on, other than what follows from the above.
Results may differ from a plain program's by a relative error of at most 0.012.
Values may be sent and summed in bfloat16 or wider, within the bound.
A program may use at most 192 MiB of HBM per device.

v0:
```python
from functools import partial
import jax
import jax.numpy as jnp
from jax import lax
from jax.sharding import PartitionSpec as P

D = 768
HEADS = 12
HD = 64
LEN = 16
PATCHES = 50


def layer_norm(tensor, norm_gain, norm_shift):
    centred = tensor - jnp.mean(tensor, axis=-1, keepdims=True)
    variance = jnp.mean(centred * centred, axis=-1, keepdims=True)
    return centred * lax.rsqrt(variance + 1e-06) * norm_gain + norm_shift


def normalize(pooled):
    return pooled * lax.rsqrt(jnp.sum(pooled * pooled, axis=-1, keepdims=True) + 1e-06)


def product(left, right):
    return jnp.dot(left, right, preferred_element_type=jnp.float32)


def masked_scores(queries, key_rows, causal):
    scores = jnp.einsum(
        "gqhd,gkhd->ghqk", queries, key_rows, preferred_element_type=jnp.float32
    ) * HD ** (-0.5)
    if causal:
        places = jnp.arange(scores.shape[-1], dtype=jnp.int32)
        scores = jnp.where(places[None, :] <= places[:, None], scores, -1e30)
    return scores


def softmax_rows(scores):
    highest = jnp.max(scores, axis=-1, keepdims=True)
    weights = jnp.exp(scores - highest)
    totals = jnp.sum(weights, axis=-1, keepdims=True)
    return (weights / totals, highest + jnp.log(totals))


def attention_back(queries, key_rows, value_rows, log_totals, mixed_grad):
    scores = masked_scores(queries, key_rows, True)
    attn_probs = jnp.exp(scores - log_totals)
    probs_grad = jnp.einsum(
        "gqhd,gkhd->ghqk", mixed_grad, value_rows, preferred_element_type=jnp.float32
    )
    value_grad = jnp.einsum(
        "ghqk,gqhd->gkhd",
        attn_probs.astype(jnp.bfloat16),
        mixed_grad,
        preferred_element_type=jnp.float32,
    )
    inner_sum = jnp.sum(attn_probs * probs_grad, axis=-1, keepdims=True)
    score_grad = (attn_probs * (probs_grad - inner_sum)).astype(jnp.bfloat16)
    query_grad = jnp.einsum(
        "ghqk,gkhd->gqhd", score_grad, key_rows, preferred_element_type=jnp.float32
    ) * HD ** (-0.5)
    key_grad = jnp.einsum(
        "ghqk,gqhd->gkhd", score_grad, queries, preferred_element_type=jnp.float32
    ) * HD ** (-0.5)
    return (query_grad, key_grad, value_grad)


def image_embed(stored_picture_patches, frozen):
    (
        picture_lookup_coefficients,
        picture_address_coefficients,
        picture_content_coefficients,
        picture_mixer_exit,
        picture_perceptron_entry,
        picture_perceptron_exit,
    ) = frozen
    tokens = stored_picture_patches.astype(jnp.float32)
    examples = tokens.shape[0] // PATCHES
    normed = layer_norm(tokens, 1.0, 0.0).astype(jnp.bfloat16)
    grid_shape = (examples, PATCHES, HEADS, HD)
    queries = product(normed, picture_lookup_coefficients).astype(jnp.bfloat16).reshape(grid_shape)
    key_rows = (
        product(normed, picture_address_coefficients).astype(jnp.bfloat16).reshape(grid_shape)
    )
    value_rows = (
        product(normed, picture_content_coefficients).astype(jnp.bfloat16).reshape(grid_shape)
    )
    attn_probs, unused_totals = softmax_rows(masked_scores(queries, key_rows, False))
    mixed_heads = jnp.einsum(
        "ghqk,gkhd->gqhd",
        attn_probs.astype(jnp.bfloat16),
        value_rows,
        preferred_element_type=jnp.float32,
    )
    mixed_heads = mixed_heads.reshape(examples * PATCHES, D).astype(jnp.bfloat16)
    middle = tokens + product(mixed_heads, picture_mixer_exit)
    normed_two = layer_norm(middle, 1.0, 0.0).astype(jnp.bfloat16)
    hidden_act = jax.nn.gelu(
        product(normed_two, picture_perceptron_entry), approximate=True
    ).astype(jnp.bfloat16)
    output = middle + product(hidden_act, picture_perceptron_exit)
    return normalize(jnp.mean(output.reshape(examples, PATCHES, D), axis=1)).astype(jnp.bfloat16)


def embed(block_out):
    return normalize(jnp.mean(block_out.reshape(-1, LEN, D), axis=1))


def body(
    sentence_entry_words,
    sentence_present_marks,
    picture_present_marks,
    matched_picture_positions,
    stored_picture_patches,
    log_logit_multiplier,
    leading_standardizer_stretch,
    leading_standardizer_shift,
    lookup_coefficients,
    lookup_offset,
    address_coefficients,
    content_coefficients,
    content_offset,
    mixer_exit_coefficients,
    mixer_exit_offset,
    trailing_standardizer_stretch,
    trailing_standardizer_shift,
    perceptron_entry_coefficients,
    perceptron_inner_offset,
    perceptron_exit_coefficients,
    perceptron_exit_offset,
    picture_lookup_coefficients,
    picture_address_coefficients,
    picture_content_coefficients,
    picture_mixer_exit,
    picture_perceptron_entry,
    picture_perceptron_exit,
):
    own_count = sentence_present_marks.shape[0]
    mp_count = lax.axis_size("mp")
    rank = lax.axis_index("mp")
    text_mask, image_mask = (
        lax.all_gather(
            sentence_present_marks.astype(jnp.float32), ("dp", "mp"), axis=0, tiled=True
        ),
        lax.all_gather(picture_present_marks.astype(jnp.float32), ("dp", "mp"), axis=0, tiled=True),
    )
    wide = partial(lax.all_gather, axis_name="mp", axis=1, tiled=True)
    tall = partial(lax.all_gather, axis_name="mp", axis=0, tiled=True)
    w_q, w_k, w_v, w_o = (
        wide(lookup_coefficients),
        wide(address_coefficients),
        wide(content_coefficients),
        tall(mixer_exit_coefficients),
    )
    w_h, w_p = (wide(perceptron_entry_coefficients), tall(perceptron_exit_coefficients))
    b_q, b_v, b_h = (tall(lookup_offset), tall(content_offset), tall(perceptron_inner_offset))
    image_half = image_embed(
        stored_picture_patches,
        (
            picture_lookup_coefficients,
            picture_address_coefficients,
            picture_content_coefficients,
            picture_mixer_exit,
            picture_perceptron_entry,
            picture_perceptron_exit,
        ),
    )
    all_image = lax.all_gather(image_half, ("dp", "mp"), axis=0, tiled=True)
    tokens = sentence_entry_words.astype(jnp.float32)
    all_rows = tokens.shape[0]
    normed_one, norm_one_back = jax.vjp(
        layer_norm, tokens, leading_standardizer_stretch, leading_standardizer_shift
    )
    normed_one = normed_one.astype(jnp.bfloat16)
    grid_shape = (all_rows // LEN, LEN, HEADS, HD)
    queries = (product(normed_one, w_q) + b_q).astype(jnp.bfloat16).reshape(grid_shape)
    key_rows = product(normed_one, w_k).astype(jnp.bfloat16).reshape(grid_shape)
    value_rows = (product(normed_one, w_v) + b_v).astype(jnp.bfloat16).reshape(grid_shape)
    attn_probs, log_totals = softmax_rows(masked_scores(queries, key_rows, True))
    mixed_heads = jnp.einsum(
        "ghqk,gkhd->gqhd",
        attn_probs.astype(jnp.bfloat16),
        value_rows,
        preferred_element_type=jnp.float32,
    )
    mixed_heads = mixed_heads.reshape(all_rows, D).astype(jnp.bfloat16)
    middle = tokens + product(mixed_heads, w_o) + mixer_exit_offset
    normed_two, norm_two_back = jax.vjp(
        layer_norm, middle, trailing_standardizer_stretch, trailing_standardizer_shift
    )
    normed_two = normed_two.astype(jnp.bfloat16)
    hidden_pre = product(normed_two, w_h) + b_h
    hidden_act, gelu_back = jax.vjp(partial(jax.nn.gelu, approximate=True), hidden_pre)
    hidden_act = hidden_act.astype(jnp.bfloat16)
    output = middle + product(hidden_act, w_p) + perceptron_exit_offset
    text_emb, embed_back = jax.vjp(embed, output)
    text_half = text_emb.astype(jnp.bfloat16)
    everyone = text_mask.shape[0]
    order = jnp.arange(everyone, dtype=jnp.int32)
    offset = lax.axis_index(("dp", "mp")) * own_count
    own_pair = lax.dynamic_slice_in_dim(matched_picture_positions, offset, own_count, 0)
    own_text = sentence_present_marks.astype(jnp.float32)
    hits = (order[None, :] == own_pair[:, None]).astype(jnp.float32)
    text_weight = own_text * jnp.sum(hits * image_mask[None, :], axis=1)
    inverse = jnp.zeros((everyone,), jnp.int32).at[matched_picture_positions].set(order)
    image_weight = image_mask * text_mask[inverse]
    logit_multiplier = jnp.exp(log_logit_multiplier[0])
    logits = logit_multiplier * jnp.einsum(
        "id,jd->ij", text_half, all_image, preferred_element_type=jnp.float32
    )
    weights = jnp.exp(logits)
    row_weights = weights * image_mask[None, :]
    row_total = jnp.sum(row_weights, axis=1)
    column_weights = weights * own_text[:, None]
    column_total = lax.psum(jnp.sum(column_weights, axis=0), ("dp", "mp"))
    pair_total = jnp.sum(image_weight)
    safe_row = jnp.where(row_total > 0, row_total, 1.0)
    safe_column = jnp.where(column_total > 0, column_total, 1.0)
    hit_logit = jnp.sum(hits * logits, axis=1)
    column_part = 0.5 * jnp.sum(image_weight * jnp.log(safe_column))
    total_part = 0.5 * jnp.sum(text_weight * jnp.log(safe_row)) - jnp.sum(text_weight * hit_logit)
    row_grad = 0.5 * text_weight[:, None] * (row_weights / safe_row[:, None] - hits)
    column_grad = 0.5 * image_weight[None, :] * (column_weights / safe_column[None, :] - hits)
    temp_part = jnp.sum((row_grad + column_grad) * logits)
    text_grad = product((logit_multiplier * row_grad).astype(jnp.bfloat16), all_image) + product(
        (logit_multiplier * column_grad).astype(jnp.bfloat16), all_image
    )
    token_grad = embed_back(text_grad)[0]
    proj_bias_grad = jnp.sum(token_grad, axis=0)
    grad_rows = token_grad.astype(jnp.bfloat16)
    w_proj_grad = jnp.einsum("rf,rd->fd", hidden_act, grad_rows, preferred_element_type=jnp.float32)
    active_grad = jnp.einsum("rd,fd->rf", grad_rows, w_p, preferred_element_type=jnp.float32)
    hidden_grad = gelu_back(active_grad)[0].astype(jnp.bfloat16)
    w_hidden_grad = jnp.einsum(
        "rd,rf->df", normed_two, hidden_grad, preferred_element_type=jnp.float32
    )
    hidden_bias_grad = jnp.sum(hidden_grad.astype(jnp.float32), axis=0)
    normed_two_grad = jnp.einsum("rf,df->rd", hidden_grad, w_h, preferred_element_type=jnp.float32)
    norm_two_grads = norm_two_back(normed_two_grad)
    middle_grad = token_grad + norm_two_grads[0]
    attn_bias_grad = jnp.sum(middle_grad, axis=0)
    attn_grad_rows = middle_grad.astype(jnp.bfloat16)
    w_attn_out_grad = jnp.einsum(
        "rk,rd->kd", mixed_heads, attn_grad_rows, preferred_element_type=jnp.float32
    )
    mixed_grad = jnp.einsum("rd,kd->rk", attn_grad_rows, w_o, preferred_element_type=jnp.float32)
    mixed_grad = mixed_grad.astype(jnp.bfloat16).reshape(grid_shape)
    query_grad, key_grad, value_grad = attention_back(
        queries, key_rows, value_rows, log_totals, mixed_grad
    )
    query_grad = query_grad.reshape(all_rows, D).astype(jnp.bfloat16)
    key_grad = key_grad.reshape(all_rows, D).astype(jnp.bfloat16)
    value_grad = value_grad.reshape(all_rows, D).astype(jnp.bfloat16)
    back = partial(jnp.einsum, "rd,rk->dk", normed_one, preferred_element_type=jnp.float32)
    w_query_grad, w_key_grad, w_value_grad = (back(query_grad), back(key_grad), back(value_grad))
    query_bias_grad = jnp.sum(query_grad.astype(jnp.float32), axis=0)
    value_bias_grad = jnp.sum(value_grad.astype(jnp.float32), axis=0)
    down = partial(jnp.einsum, "rk,dk->rd", preferred_element_type=jnp.float32)
    normed_one_grad = down(query_grad, w_q) + down(key_grad, w_k) + down(value_grad, w_v)
    norm_one_grads = norm_one_back(normed_one_grad)
    text_in_grad = middle_grad + norm_one_grads[0]

    def share(grad, axis):
        part = lax.psum_scatter(grad.astype(jnp.bfloat16), "mp", scatter_dimension=axis, tiled=True)
        return lax.psum(part, "dp").astype(jnp.float32)

    shared = lax.psum(
        (
            total_part,
            temp_part,
            norm_one_grads[1],
            norm_one_grads[2],
            attn_bias_grad,
            norm_two_grads[1],
            norm_two_grads[2],
            proj_bias_grad,
            query_bias_grad,
            value_bias_grad,
            hidden_bias_grad,
        ),
        ("dp", "mp"),
    )
    loss = jnp.reshape((shared[0] + column_part) / pair_total, (1,))

    def own(vector):
        return lax.dynamic_slice_in_dim(
            vector, rank * (vector.shape[0] // mp_count), vector.shape[0] // mp_count, 0
        )

    return (
        loss,
        output.astype(jnp.bfloat16),
        text_in_grad,
        jnp.reshape(shared[1], (1,)),
        shared[2],
        shared[3],
        share(w_query_grad, 1),
        own(shared[8]),
        share(w_key_grad, 1),
        share(w_value_grad, 1),
        own(shared[9]),
        share(w_attn_out_grad, 0),
        shared[4],
        shared[5],
        shared[6],
        share(w_hidden_grad, 1),
        own(shared[10]),
        share(w_proj_grad, 0),
        shared[7],
    )


def solution(mesh):
    in_specs = (
        P(("dp", "mp"), None),
        P(("dp", "mp")),
        P(("dp", "mp")),
        P(),
        P(("dp", "mp"), None),
        P(),
        P(),
        P(),
        P(None, "mp"),
        P("mp"),
        P(None, "mp"),
        P(None, "mp"),
        P("mp"),
        P("mp", None),
        P(),
        P(),
        P(),
        P(None, "mp"),
        P("mp"),
        P("mp", None),
        P(),
        P(),
        P(),
        P(),
        P(),
        P(),
        P(),
    )
    out_specs = (
        P(),
        P(("dp", "mp"), None),
        P(("dp", "mp"), None),
        P(),
        P(),
        P(),
        P(None, "mp"),
        P("mp"),
        P(None, "mp"),
        P(None, "mp"),
        P("mp"),
        P("mp", None),
        P(),
        P(),
        P(),
        P(None, "mp"),
        P("mp"),
        P("mp", None),
        P(),
    )
    return jax.shard_map(body, mesh=mesh, in_specs=in_specs, out_specs=out_specs, check_vma=False)
```

profile of v0, /device:TPU:0, one launch (start us, length us, event | category | flops | bytes accessed | tf_op | source)
XLA Modules:
  0.0 737.5 jit_solution(3353801001150994818)
XLA Ops:
  18.3 8.5 %reshape.272 = bf16[32,50,12,64]{3,2,1,0:T(8,128)(2,1)} reshape(bf16[1600,768]{1,0:T(8,128)(2,1)} %convolution_convert_fusion.2) | data formatting | bytes 4915200 | tf_op jit(solution)/shard_map/reshape | solution.py:83
  26.8 5.4 convolution_convert_fusion.3
  32.2 8.6 %reshape.271 = bf16[32,50,12,64]{3,2,1,0:T(8,128)(2,1)} reshape(bf16[1600,768]{1,0:T(8,128)(2,1)} %convolution_convert_fusion.3) | data formatting | bytes 4915200 | tf_op jit(solution)/shard_map/reshape | solution.py:81
  40.8 11.8 %fusion.26 = f32[32,12,50,50]{2,3,1,0:T(8,128)} fusion(bf16[32,50,12,64]{3,2,1,0:T(8,128)(2,1)} %reshape.272, bf16[32,50,12,64]{3,2,1,0:T(8,128)(2,1)} %reshape.271), kind=kOutput, calls=%fused_computation.35 | convolution fusion | flops 122880000 | bytes 8755200 | tf_op jit(solution)/shard_map/gqhd,gkhd->ghqk/dot_general | solution.py:29
  52.7 15.2 %fusion.112 = (f32[32,12,50]{2,1,0:T(8,128)S(1)}, f32[32,12,50,50]{2,3,1,0:T(8,128)}) fusion(f32[32,12,50,50]{2,3,1,0:T(8,128)} %fusion.26), kind=kOutput, calls=%fused_computation.197 | output fusion | flops 3840049 | bytes 7756800 | tf_op jit(solution)/shard_map/sub | solution.py:40
  71.5 8.5 %reshape.270 = bf16[32,50,12,64]{3,2,1,0:T(8,128)(2,1)} reshape(bf16[1600,768]{1,0:T(8,128)(2,1)} %convolution_convert_fusion.4) | data formatting | bytes 4915200 | tf_op jit(solution)/shard_map/reshape | solution.py:86
  80.0 9.3 %convert_bitcast_fusion = bf16[32,50,12,64]{3,1,2,0:T(8,128)(2,1)} fusion(f32[32,12,50,50]{2,3,1,0:T(8,128)} %get-tuple-element.69, f32[32,12,50]{2,1,0:T(8,128)S(1)} %get-tuple-element.68, bf16[32,50,12,64]{3,2,1,0:T(8,128)(2,1)} %reshape.270), kind=kOutput, calls=%fused_computation.39 | convolution fusion | flops 126028800 | bytes 8832000 | tf_op jit(solution)/shard_map/ghqk,gkhd->gqhd/dot_general | solution.py:89
  89.3 9.6 %copy.116 = bf16[32,50,12,64]{1,0,3,2:T(8,128)(2,1)} copy(bf16[32,50,12,64]{3,1,2,0:T(8,128)(2,1)} %convert_bitcast_fusion) | data formatting | bytes 4915200 | tf_op jit(solution)/shard_map/convert_element_type | solution.py:95
  98.9 11.7 %convert_element_type.211 = bf16[1600,768]{0,1:T(8,128)(2,1)} reshape(bf16[32,50,12,64]{1,0,3,2:T(8,128)(2,1)} %copy.116) | data formatting | bytes 4915200 | tf_op jit(solution)/shard_map/convert_element_type | solution.py:95
  110.7 4.8 fusion.113
  117.7 23.4 %fusion.34 = f32[1600,768]{1,0:T(8,128)} fusion(f32[1600,768]{1,0:T(8,128)} %copy-done.14, bf16[3072,768]{1,0:T(8,128)(2,1)} %param.53, bf16[768,3072]{1,0:T(8,128)(2,1)} %param.52, f32[1600]{0:T(1024)S(1)} %add_rsqrt_fusion, f32[1600]{0:T(1024)S(1)} %broadcast_multiply_fusion), kind=kOutput, calls=%fused_computation.48 | convolution fusion | flops 15148646400 | bytes 19280384 | tf_op jit(solution)/shard_map/dot_general | solution.py:25
  141.1 5.4 reshape.231
  151.5 42.6 %all-reduce = f32[1024]{0:T(1024)S(1)} all-reduce(f32[1024]{0:T(1024)S(1)} %convert_dynamic-update-slice_fusion), channel_id=1, replica_groups=mesh['dp'=8,'mp'=4] {'dp','mp'}, use_global_device_ids=true, to_apply=%add | all-reduce | flops 1024 | bytes 8192
  195.9 5.5 all-gather
  202.2 4.3 scatter_custom_fusion
  208.2 8.0 %all-reduce.6 = (f32[768]{0:T(1024)S(1)}, f32[768]{0:T(1024)S(1)}) all-reduce(f32[768]{0:T(1024)S(1)} %dynamic-update-slice.2, f32[768]{0:T(1024)S(1)} %dynamic-update-slice.1), channel_id=1, replica_groups=mesh['dp'=8,'mp'=4] {'mp'}, use_global_device_ids=true, to_apply=%add.2 | all-reduce | flops 1536 | bytes 12288
  237.9 4.1 convert_element_type.199
  246.8 8.2 %fusion.99 = f32[512,3072]{1,0:T(8,128)} fusion(bf16[768,3072]{1,0:T(8,128)(2,1)} %all-gather.17.cloned.1.call-done, f32[512,768]{1,0:T(8,128)} %copy-done.11, f32[768]{0:T(1024)S(1)} %copy-done.85, f32[768]{0:T(1024)S(1)} %copy-done.65, f32[512]{0:T(512)S(1)} %fusion.92, f32[512]{0:T(512)S(1)} %broadcast_multiply_fusion.3), kind=kOutput, calls=%fused_computation.194 | convolution fusion | flops 2417885184 | bytes 12593152 | tf_op jit(solution)/shard_map/dot_general | solution.py:25
  255.1 9.6 %bitcast_reduce_fusion = (f32[32,768]{1,0:T(8,128)S(1)}, bf16[512,768]{1,0:T(8,128)(2,1)}) fusion(f32[768]{0:T(1024)S(1)} %copy-done.82, f32[512,768]{1,0:T(8,128)} %copy-done.11, bf16[3072,768]{1,0:T(8,128)(2,1)} %all-gather.19.cloned.1.call-done, f32[512,3072]{1,0:T(8,128)} %fusion.99, f32[3072]{0:T(1024)S(1)} %bitcast.68), kind=kOutput, calls=%fused_computation.87 | convolution fusion | flops 2433196032 | bytes 13483008 | tf_op jit(solution)/shard_map/dot_general | solution.py:25
  271.1 39.8 %all-reduce.5 = (f32[1024]{0:T(1024)}, f32[1024]{0:T(1024)S(1)}) all-reduce(f32[1024]{0:T(1024)} %get-tuple-element.28, f32[1024]{0:T(1024)} %copy-done.47), channel_id=1, replica_groups=mesh['dp'=8,'mp'=4] {'dp','mp'}, use_global_device_ids=true, to_apply=%region_24.25 | all-reduce | flops 2048 | bytes 16384 | tf_op jit(solution)/shard_map/psum | solution.py:215
  310.8 9.0 %gather_fusion = f32[1024]{0:T(1024)} fusion(f32[1024]{0:T(1024)S(1)} %get-tuple-element.47, s32[1024]{0:T(1024)} %fusion.88), kind=kCustom, calls=%fused_computation | custom fusion | bytes 12288 | tf_op jit(solution)/shard_map/gather | solution.py:206
  325.0 10.2 %convert_reduce_fusion.1 = (f32[3072]{0:T(1024)}, bf16[512,3072]{1,0:T(8,128)(2,1)S(1)}) fusion(f32[512,3072]{1,0:T(8,128)} %fusion.99, f32[3072]{0:T(1024)S(1)} %bitcast.69, bf16[512,768]{1,0:T(8,128)(2,1)S(1)} %bitcast_convert_fusion, bf16[3072,768]{1,0:T(8,128)(2,1)} %all-gather.19.cloned.1.call-done), kind=kOutput, calls=%fused_computation.30 | convolution fusion | flops 2452091904 | bytes 14966784 | tf_op jit(solution)/shard_map/rd,fd->rf/dot_general | solution.py:232
  368.3 3.9 convert_element_type.229
  387.6 6.5 convolution_convert_fusion.1
  395.3 8.8 %convolution_convert_fusion = bf16[3072,768]{1,0:T(8,128)(2,1)} fusion(bf16[512,768]{1,0:T(8,128)(2,1)S(1)} %copy-done.29, f32[512,3072]{1,0:T(8,128)} %fusion.99, f32[3072]{0:T(1024)S(1)} %bitcast.70), kind=kOutput, calls=%fused_computation.42 | convolution fusion | flops 2434007040 | bytes 11808768 | tf_op jit(solution)/shard_map/rf,rd->fd/dot_general | solution.py:231
  404.2 13.8 %reduce-scatter.9.cloned.1.call-done = bf16[768,192]{0,1:T(8,128)(2,1)} async-done(((bf16[768,768]{0,1:T(8,128)(2,1)}), bf16[768,192]{0,1:T(8,128)(2,1)}) %reduce-scatter.9.cloned.1.call-update) | async-done | bytes 294928 | tf_op jit(solution)/shard_map/reduce_scatter | solution.py:264
  418.0 28.6 %reduce-scatter.11.cloned.1.call-done = bf16[768,192]{0,1:T(8,128)(2,1)} async-done(((bf16[768,768]{0,1:T(8,128)(2,1)}), bf16[768,192]{0,1:T(8,128)(2,1)}) %reduce-scatter.11.cloned.1.call-update) | async-done | bytes 294928 | tf_op jit(solution)/shard_map/reduce_scatter | solution.py:264
  446.6 28.2 %reduce-scatter.13.cloned.1.call-done = bf16[192,768]{1,0:T(8,128)(2,1)} async-done(((bf16[768,768]{1,0:T(8,128)(2,1)}), bf16[192,768]{1,0:T(8,128)(2,1)}) %reduce-scatter.13.cloned.1.call-update) | async-done | bytes 294928 | tf_op jit(solution)/shard_map/reduce_scatter | solution.py:264
  474.9 50.3 %reduce-scatter.15.cloned.1.call-done = bf16[768,768]{1,0:T(8,128)(2,1)} async-done(((bf16[768,3072]{1,0:T(8,128)(2,1)}), bf16[768,768]{1,0:T(8,128)(2,1)}) %reduce-scatter.15.cloned.1.call-update) | async-done | bytes 1179664 | tf_op jit(solution)/shard_map/reduce_scatter | solution.py:264
  525.1 50.5 %reduce-scatter.17.cloned.1.call-done = bf16[768,768]{1,0:T(8,128)(2,1)} async-done(((bf16[3072,768]{1,0:T(8,128)(2,1)}), bf16[768,768]{1,0:T(8,128)(2,1)}) %reduce-scatter.17.cloned.1.call-update) | async-done | bytes 1179664 | tf_op jit(solution)/shard_map/reduce_scatter | solution.py:264
  587.8 45.1 %all-reduce.4 = (f32[]{:T(128)}, f32[1]{0:T(128)}, f32[768]{0:T(1024)}, f32[768]{0:T(1024)}, f32[768]{0:T(1024)S(1)}, /*index=5*/f32[768]{0:T(1024)S(1)}, f32[76...) all-reduce(f32[]{:T(128)S(6)} %sub.88, ...), channel_id=1, replica_groups=mesh['dp'=8,'mp'=4] {'dp','mp'}, use_global_device_ids=true, to_apply=%region_21.22 | all-reduce | flops 9218 | bytes 73744 | tf_op jit(solution)/shard_map/psum | solution.py:267
  636.9 83.1 %all-reduce.10.cloned.1.call-done = (bf16[768,192]{0,1:T(8,128)(2,1)}, bf16[768,192]{0,1:T(8,128)(2,1)}, bf16[768,192]{0,1:T(8,128)(2,1)}, bf16[192,768]{1,0:T(8...) async-done(((bf16[768,192]{0,1:T(8,128)(2,1)}, bf16[768,192]{0,1:T(8,128)(2,1)}, bf16[768,192]{0,1:T(8,128)(2,1)}, bf16[192,768]{1,0:T(8,128)(2,1)}, ...) | async-done | bytes 3538960 | tf_op jit(solution)/shard_map/psum | solution.py:265
  (321 shorter events, 133.8 us)
Async XLA Ops:
  7.2 103.5 %copy-start = (bf16[768,768]{1,0:T(8,128)(2,1)S(1)}, bf16[768,768]{1,0:T(8,128)(2,1)}, u32[]{:S(2)}) copy-start(bf16[768,768]{1,0:T(8,128)(2,1)} %param.51) | copy-start | bytes 3538948
  7.2 209.1 %all-gather.13.cloned.1.call-start = ((), (), s32[]{:S(2)}) async-start(), calls=%async_computation.8 | async-start | bytes 1474560 | tf_op jit(solution)/shard_map/all_gather | solution.py:151
  7.9 212.8 %all-gather.11.cloned.1.call-start = ((), (), s32[]{:S(2)}) async-start(), calls=%async_computation.7 | async-start | bytes 1474560 | tf_op jit(solution)/shard_map/all_gather | solution.py:150
  8.7 216.5 %all-gather.9.cloned.1.call-start = ((), (), s32[]{:S(2)}) async-start(), calls=%async_computation.6 | async-start | bytes 1474560 | tf_op jit(solution)/shard_map/all_gather | solution.py:152
  9.4 232.6 %all-gather.15.cloned.1.call-start = ((), (), s32[]{:S(2)}) async-start(), calls=%async_computation.9 | async-start | bytes 1474560 | tf_op jit(solution)/shard_map/all_gather | solution.py:153
  10.0 236.8 %all-gather.17.cloned.1.call-start = ((), (), s32[]{:S(2)}) async-start(), calls=%async_computation.10 | async-start | bytes 5898240 | tf_op jit(solution)/shard_map/all_gather | solution.py:155
  10.6 244.4 %all-gather.19.cloned.1.call-start = ((), (), s32[]{:S(2)}) async-start(), calls=%async_computation.11 | async-start | bytes 5898240 | tf_op jit(solution)/shard_map/all_gather | solution.py:155
  11.2 254.8 %all-gather.21.cloned.1.call-start = ((), (), s32[]{:S(2)}) async-start(), calls=%async_computation.12 | async-start | bytes 1622016 | tf_op jit(solution)/shard_map/all_gather | solution.py:168
  52.7 15.2 %copy-start.8 = (bf16[1600,768]{1,0:T(8,128)(2,1)S(1)}, bf16[1600,768]{1,0:T(8,128)(2,1)}, u32[]{:S(2)}) copy-start(bf16[1600,768]{1,0:T(8,128)(2,1)} %param.31) | copy-start | bytes 7372804
  52.7 15.2 %copy-start.79 = (bf16[768,768]{1,0:T(8,128)(2,1)S(1)}, bf16[768,768]{1,0:T(8,128)(2,1)}, u32[]{:S(2)}) copy-start(bf16[768,768]{1,0:T(8,128)(2,1)} %param.50) | copy-start | bytes 3538948
  146.5 47.7 %copy-start.64 = (s32[1024]{0:T(1024)S(1)}, s32[1024]{0:T(1024)}, u32[]{:S(2)}) copy-start(s32[1024]{0:T(1024)} %param.30) | copy-start | bytes 12292
  146.5 48.3 %copy-start.2 = (bf16[512,768]{1,0:T(8,128)(2,1)S(1)}, bf16[512,768]{1,0:T(8,128)(2,1)}, u32[]{:S(2)}) copy-start(bf16[512,768]{1,0:T(8,128)(2,1)} %param.27) | copy-start | bytes 2359300
  146.5 48.8 %copy-start.88 = (u32[32]{0:T(128)S(1)}, u32[32]{0:T(128)}, u32[]{:S(2)}) copy-start(u32[32]{0:T(128)} %constant.94) | copy-start | bytes 388
  146.5 49.4 %copy-start.63 = (f32[768]{0:T(1024)S(1)}, f32[768]{0:T(1024)}, u32[]{:S(2)}) copy-start(f32[768]{0:T(1024)} %param.45) | copy-start | bytes 9220
  146.5 61.2 %copy-start.72 = (f32[192]{0:T(256)S(1)}, f32[192]{0:T(256)}, u32[]{:S(2)}) copy-start(f32[192]{0:T(256)} %param.36) | copy-start | bytes 2308
  146.5 61.5 %copy-start.73 = (f32[192]{0:T(256)S(1)}, f32[192]{0:T(256)}, u32[]{:S(2)}) copy-start(f32[192]{0:T(256)} %param.39) | copy-start | bytes 2308
  146.6 69.7 %copy-start.34 = (f32[768]{0:T(1024)S(1)}, f32[768]{0:T(1024)}, u32[]{:S(2)}) copy-start(f32[768]{0:T(1024)} %param.33) | copy-start | bytes 9220
  146.6 69.7 %copy-start.83 = (f32[768]{0:T(1024)S(1)}, f32[768]{0:T(1024)}, u32[]{:S(2)}) copy-start(f32[768]{0:T(1024)} %param.34) | copy-start | bytes 9220
  150.7 253.6 %reduce-scatter.7.cloned.1.call-start = ((), (), s32[]{:S(2)}) async-start(), calls=%async_computation.13 | async-start | bytes 1474560 | tf_op jit(solution)/shard_map/reduce_scatter | solution.py:264
  195.3 21.0 %copy-start.43 = (f32[512]{0:T(512)}, f32[512]{0:T(512)S(1)}, u32[]{:S(2)}) copy-start(f32[512]{0:T(512)S(1)} %fusion.54) | copy-start | bytes 6148
  195.3 29.9 %copy-start.39 = (f32[512]{0:T(512)}, f32[512]{0:T(512)S(1)}, u32[]{:S(2)}) copy-start(f32[512]{0:T(512)S(1)} %fusion.91) | copy-start | bytes 6148
  201.4 53.6 %copy-start.49 = (f32[4,1,768]{2,1,0:T(1,128)}, f32[4,1,768]{2,1,0:T(1,128)S(1)}, u32[]{:S(2)}) copy-start(f32[4,1,768]{2,1,0:T(1,128)S(1)} %all-gather) | copy-start | bytes 36868
  255.1 11.0 %copy-start.55 = (s32[32]{0:T(128)S(1)}, s32[32]{0:T(128)}, u32[]{:S(2)}) copy-start(s32[32]{0:T(128)} %dynamic_slice.12) | copy-start | bytes 388
  268.7 54.5 %copy-start.17 = (f32[32,1024]{1,0:T(8,128)}, f32[32,1024]{1,0:T(8,128)S(1)}, u32[]{:S(2)}) copy-start(f32[32,1024]{1,0:T(8,128)S(1)} %get-tuple-element.78) | copy-start | bytes 393220
  363.3 54.7 %reduce-scatter.9.cloned.1.call-start = ((), (), s32[]{:S(2)}) async-start(), calls=%async_computation.14 | async-start | bytes 1474560 | tf_op jit(solution)/shard_map/reduce_scatter | solution.py:264
  375.6 71.0 %reduce-scatter.11.cloned.1.call-start = ((), (), s32[]{:S(2)}) async-start(), calls=%async_computation.15 | async-start | bytes 1474560 | tf_op jit(solution)/shard_map/reduce_scatter | solution.py:264
  384.4 90.5 %reduce-scatter.13.cloned.1.call-start = ((), (), s32[]{:S(2)}) async-start(), calls=%async_computation.16 | async-start | bytes 1474560 | tf_op jit(solution)/shard_map/reduce_scatter | solution.py:264
  387.5 137.6 %reduce-scatter.15.cloned.1.call-start = ((), (), s32[]{:S(2)}) async-start(), calls=%async_computation.17 | async-start | bytes 5898240 | tf_op jit(solution)/shard_map/reduce_scatter | solution.py:264
  394.2 181.5 %reduce-scatter.17.cloned.1.call-start = ((), (), s32[]{:S(2)}) async-start(), calls=%async_computation.18 | async-start | bytes 5898240 | tf_op jit(solution)/shard_map/reduce_scatter | solution.py:264
  404.1 171.6 %copy-start.54 = (f32[12,64]{1,0:T(8,128)S(1)}, f32[12,64]{1,0:T(8,128)}, u32[]{:S(2)}) copy-start(f32[12,64]{1,0:T(8,128)} %get-tuple-element.85) | copy-start | bytes 9220
  404.1 171.7 %copy-start.31 = (bf16[512,768]{1,0:T(8,128)(2,1)S(1)}, bf16[512,768]{1,0:T(8,128)(2,1)}, u32[]{:S(2)}) copy-start(bf16[512,768]{1,0:T(8,128)(2,1)} %convert_element_type.226) | copy-start | bytes 2359300
  404.1 315.9 %all-reduce.10.cloned.1.call-start = ((), (), s32[]{:S(2)}) async-start(), calls=%async_computation.19 | async-start | bytes 7077888 | tf_op jit(solution)/shard_map/psum | solution.py:265
  (74 other events, 281.9 us)
Sparse Core Ops, SparseCore 0:
  9.6 20.1 all-gather.12
  31.3 17.4 all-gather.10
  50.4 17.4 all-gather.8
  69.2 17.4 all-gather.14
  88.1 37.4 all-gather.16
  127.0 37.9 all-gather.18
  168.4 55.1 all-gather.20
  363.4 25.7 reduce-scatter.6
  392.3 25.6 reduce-scatter.8
  421.0 25.6 reduce-scatter.10
  449.2 25.6 reduce-scatter.12
  477.2 47.8 reduce-scatter.14
  527.6 47.9 reduce-scatter.16
  579.8 140.1 all-reduce.9
where the time goes:
time: 745 us; the launch traced here: 737 us
  waiting for transfers between devices  258 us (35%)
  matrix products  160 us (21%)
  blocking collectives  141 us (19%)
  local copies, waits for them, and re-layouts  110 us (15%)
  other arithmetic  46 us (6%)
  between operations  21.1 us (3%)
    reduce_scatter x6, waiting for transfers between devices, share(): lax.psum_scatter(grad.astype(jnp.bfloat16), 'mp', scatter_dimension=axis,...  171 us
    psum x1, waiting for transfers between devices, share(): return lax.psum(part, 'dp').astype(jnp.float32)  83.1 us
    dot_general x13, matrix products, product(): return jnp.dot(left, right, preferred_element_type=jnp.float32)  71.3 us
    unnamed x2, blocking collectives  50.7 us
    psum x1, blocking collectives, body(): lax.psum((total_part, temp_part, norm_one_grads[1], norm_one_grads[2], at...  45.1 us
    psum x1, blocking collectives, body(): column_total = lax.psum(jnp.sum(column_weights, axis=0), ('dp', 'mp'))  39.8 us
    convert_element_type x2, local copies, waits for them, and re-layouts, image_embed(): mixed_heads.reshape(examples * PATCHES, D).astype(jnp.bfloat16)  21.4 us
    dot_general x2, matrix products, masked_scores(): jnp.einsum('gqhd,gkhd->ghqk', queries, key_rows, preferred_element_type=j...  15.3 us
  transfers between devices with their start and end apart: 14, of which 6 were waited for; matrix products, arithmetic and copies ran while one was open for 33% of the time, Pallas kernels for 0%

commit v1 on v0

--- a/solution.py
+++ b/solution.py
@@ -1,3 +1,4 @@
+import functools
 from functools import partial
 import jax
 import jax.numpy as jnp
@@ -9,6 +10,13 @@
 HD = 64
 LEN = 16
 PATCHES = 50
+
+
+def guide_the_knots(x_part, dev_axis):
+    return lax.all_gather(x_part, dev_axis).sum(axis=0)
+
+
+run_stops_all_by_axis = functools.partial(guide_the_knots, dev_axis="dp")
 
 
 def layer_norm(tensor, norm_gain, norm_shift):
@@ -262,7 +270,7 @@
 
     def share(grad, axis):
         part = lax.psum_scatter(grad.astype(jnp.bfloat16), "mp", scatter_dimension=axis, tiled=True)
-        return lax.psum(part, "dp").astype(jnp.float32)
+        return run_stops_all_by_axis(part).astype(jnp.float32)
 
     shared = lax.psum(
         (

time: 745 us -> 1090 us (1.46)
  waiting for transfers between devices: 258 us -> 579 us
  other arithmetic: 46 us -> 61.8 us
    all_gather x0 -> x6, waiting for transfers between devices: none -> 404 us  [guide_the_knots(): return lax.all_gather(x_part, dev_axis).sum(axis=0)]
    psum x1 -> x0, waiting for transfers between devices: 83.1 us -> none  [share(): return lax.psum(part, 'dp').astype(jnp.float32)]
    reduce_sum x0 -> x6, other arithmetic: none -> 18.8 us  [guide_the_knots(): return lax.all_gather(x_part, dev_axis).sum(axis=0)]
  transfers between devices with their start and end apart: 14 -> 19, of which waited for: 6 -> 10; matrix products, arithmetic and copies ran while one was open for 33% -> 25% of each run, Pallas kernels for 0% -> 0%
where the time goes in v1:
time: 1090 us; the launch traced here: 1080 us
  waiting for transfers between devices  579 us (53%)
  matrix products  160 us (15%)
  blocking collectives  138 us (13%)
  local copies, waits for them, and re-layouts  117 us (11%)
  other arithmetic  61.8 us (6%)
  between operations  21.3 us (2%)
    all_gather x6, waiting for transfers between devices, guide_the_knots(): return lax.all_gather(x_part, dev_axis).sum(axis=0)  404 us
    reduce_scatter x6, waiting for transfers between devices, share(): lax.psum_scatter(grad.astype(jnp.bfloat16), 'mp', scatter_dimension=axis,...  170 us
    dot_general x13, matrix products, product(): return jnp.dot(left, right, preferred_element_type=jnp.float32)  71.3 us
    unnamed x2, blocking collectives  50.2 us
    psum x1, blocking collectives, body(): lax.psum((total_part, temp_part, norm_one_grads[1], norm_one_grads[2], at...  42.1 us
    psum x1, blocking collectives, body(): column_total = lax.psum(jnp.sum(column_weights, axis=0), ('dp', 'mp'))  40.1 us
  transfers between devices with their start and end apart: 19, of which 10 were waited for; matrix products, arithmetic and copies ran while one was open for 25% of the time, Pallas kernels for 0%

profile of v1, /device:TPU:0, one launch (start us, length us, event | category | flops | bytes accessed | tf_op | source)
XLA Modules:
  0.0 1078.8 jit_solution(8029125271282272563)
XLA Ops:
  18.3 8.6 reshape.278
  32.2 8.7 reshape.277
  40.9 12.2 %fusion.26 = f32[32,12,50,50]{2,3,1,0:T(8,128)} fusion(bf16[32,50,12,64]{3,2,1,0:T(8,128)(2,1)} %reshape.278, bf16[32,50,12,64]{3,2,1,0:T(8,128)(2,1)} %reshape.277), kind=kOutput, calls=%fused_computation.35 | convolution fusion | flops 122880000 | bytes 8755200 | tf_op jit(solution)/shard_map/gqhd,gkhd->ghqk/dot_general | solution.py:37
  53.1 15.2 %fusion.112 = (f32[32,12,50]{2,1,0:T(8,128)S(1)}, f32[32,12,50,50]{2,3,1,0:T(8,128)}) fusion(f32[32,12,50,50]{2,3,1,0:T(8,128)} %fusion.26), kind=kOutput, calls=%fused_computation.200 | output fusion | flops 3840049 | bytes 7756800 | tf_op jit(solution)/shard_map/sub | solution.py:48
  71.9 8.5 reshape.276
  80.4 9.3 convert_bitcast_fusion
  89.8 9.8 copy.116
  99.5 11.8 %convert_element_type.223 = bf16[1600,768]{0,1:T(8,128)(2,1)} reshape(bf16[32,50,12,64]{1,0,3,2:T(8,128)(2,1)} %copy.116) | data formatting | bytes 4915200 | tf_op jit(solution)/shard_map/convert_element_type | solution.py:103
  118.3 23.4 %fusion.34 = f32[1600,768]{1,0:T(8,128)} fusion(f32[1600,768]{1,0:T(8,128)} %copy-done.14, bf16[3072,768]{1,0:T(8,128)(2,1)} %param.53, bf16[768,3072]{1,0:T(8,128)(2,1)} %param.52, f32[1600]{0:T(1024)S(1)} %add_rsqrt_fusion, f32[1600]{0:T(1024)S(1)} %broadcast_multiply_fusion), kind=kOutput, calls=%fused_computation.48 | convolution fusion | flops 15148646400 | bytes 19280384 | tf_op jit(solution)/shard_map/dot_general | solution.py:33
  152.2 42.2 %all-reduce = f32[1024]{0:T(1024)S(1)} all-reduce(f32[1024]{0:T(1024)S(1)} %convert_dynamic-update-slice_fusion), channel_id=1, replica_groups=mesh['dp'=8,'mp'=4] {'dp','mp'}, use_global_device_ids=true, to_apply=%add | all-reduce | flops 1024 | bytes 8192
  196.1 5.5 all-gather.6
  208.4 8.0 all-reduce.6
  247.0 8.2 fusion.99
  255.2 9.6 bitcast_reduce_fusion.3
  271.2 40.1 %all-reduce.5 = (f32[1024]{0:T(1024)}, f32[1024]{0:T(1024)S(1)}) all-reduce(f32[1024]{0:T(1024)} %get-tuple-element.28, f32[1024]{0:T(1024)} %copy-done.44), channel_id=1, replica_groups=mesh['dp'=8,'mp'=4] {'dp','mp'}, use_global_device_ids=true, to_apply=%region_24.25 | all-reduce | flops 2048 | bytes 16384 | tf_op jit(solution)/shard_map/psum | solution.py:223
  311.3 9.0 gather_fusion
  325.4 10.2 convert_reduce_fusion.1
  388.2 6.5 convolution_convert_fusion.1
  395.9 8.9 convolution_convert_fusion
  405.4 13.0 %reduce-scatter.9.cloned.1.call-done = bf16[768,192]{0,1:T(8,128)(2,1)} async-done(((bf16[768,768]{0,1:T(8,128)(2,1)}), bf16[768,192]{0,1:T(8,128)(2,1)}) %reduce-scatter.9.cloned.1.call-update) | async-done | bytes 294928 | tf_op jit(solution)/shard_map/reduce_scatter | solution.py:272
  418.5 28.6 %reduce-scatter.11.cloned.1.call-done = bf16[768,192]{0,1:T(8,128)(2,1)} async-done(((bf16[768,768]{0,1:T(8,128)(2,1)}), bf16[768,192]{0,1:T(8,128)(2,1)}) %reduce-scatter.11.cloned.1.call-update) | async-done | bytes 294928 | tf_op jit(solution)/shard_map/reduce_scatter | solution.py:272
  447.2 28.2 %reduce-scatter.13.cloned.1.call-done = bf16[192,768]{1,0:T(8,128)(2,1)} async-done(((bf16[768,768]{1,0:T(8,128)(2,1)}), bf16[192,768]{1,0:T(8,128)(2,1)}) %reduce-scatter.13.cloned.1.call-update) | async-done | bytes 294928 | tf_op jit(solution)/shard_map/reduce_scatter | solution.py:272
  475.4 50.2 %reduce-scatter.15.cloned.1.call-done = bf16[768,768]{1,0:T(8,128)(2,1)} async-done(((bf16[768,3072]{1,0:T(8,128)(2,1)}), bf16[768,768]{1,0:T(8,128)(2,1)}) %reduce-scatter.15.cloned.1.call-update) | async-done | bytes 1179664 | tf_op jit(solution)/shard_map/reduce_scatter | solution.py:272
  525.6 50.4 %reduce-scatter.17.cloned.1.call-done = bf16[768,768]{1,0:T(8,128)(2,1)} async-done(((bf16[3072,768]{1,0:T(8,128)(2,1)}), bf16[768,768]{1,0:T(8,128)(2,1)}) %reduce-scatter.17.cloned.1.call-update) | async-done | bytes 1179664 | tf_op jit(solution)/shard_map/reduce_scatter | solution.py:272
  588.2 42.1 %all-reduce.4 = (f32[]{:T(128)}, f32[1]{0:T(128)}, f32[768]{0:T(1024)}, f32[768]{0:T(1024)}, f32[768]{0:T(1024)S(1)}, /*index=5*/f32[768]{0:T(1024)S(1)}, f32[76...) all-reduce(f32[]{:T(128)S(6)} %sub.88, ...), channel_id=1, replica_groups=mesh['dp'=8,'mp'=4] {'dp','mp'}, use_global_device_ids=true, to_apply=%region_21.22 | all-reduce | flops 9218 | bytes 73744 | tf_op jit(solution)/shard_map/psum | solution.py:275
  639.0 44.0 %all-gather.37.cloned.1.call-done = bf16[6144,192]{0,1:T(8,128)(2,1)} async-done(((bf16[768,192]{0,1:T(8,128)(2,1)}), bf16[6144,192]{0,1:T(8,128)(2,1)}) %all-gather.37.cloned.1.call-update) | async-done | bytes 2359312 | tf_op jit(solution)/shard_map/all_gather | solution.py:16
  687.9 47.7 %all-gather.39.cloned.1.call-done = bf16[6144,192]{0,1:T(8,128)(2,1)} async-done(((bf16[768,192]{0,1:T(8,128)(2,1)}), bf16[6144,192]{0,1:T(8,128)(2,1)}) %all-gather.39.cloned.1.call-update) | async-done | bytes 2359312 | tf_op jit(solution)/shard_map/all_gather | solution.py:16
  740.5 47.4 %all-gather.41.cloned.1.call-done = bf16[1536,768]{1,0:T(8,128)(2,1)} async-done(((bf16[192,768]{1,0:T(8,128)(2,1)}), bf16[1536,768]{1,0:T(8,128)(2,1)}) %all-gather.41.cloned.1.call-update) | async-done | bytes 2359312 | tf_op jit(solution)/shard_map/all_gather | solution.py:16
  790.8 134.9 %all-gather.43.cloned.1.call-done = bf16[6144,768]{1,0:T(8,128)(2,1)} async-done(((bf16[768,768]{1,0:T(8,128)(2,1)}), bf16[6144,768]{1,0:T(8,128)(2,1)}) %all-gather.43.cloned.1.call-update) | async-done | bytes 9437200 | tf_op jit(solution)/shard_map/all_gather | solution.py:16
  925.7 5.7 reduce_sum.496
  933.0 130.3 %all-gather.45.cloned.1.call-done = bf16[6144,768]{1,0:T(8,128)(2,1)} async-done(((bf16[768,768]{1,0:T(8,128)(2,1)}), bf16[6144,768]{1,0:T(8,128)(2,1)}) %all-gather.45.cloned.1.call-update) | async-done | bytes 9437200 | tf_op jit(solution)/shard_map/all_gather | solution.py:16
  1063.3 5.8 reduce_sum.498
  (339 shorter events, 173.6 us)
Async XLA Ops:
  7.2 104.2 %copy-start = (bf16[768,768]{1,0:T(8,128)(2,1)S(1)}, bf16[768,768]{1,0:T(8,128)(2,1)}, u32[]{:S(2)}) copy-start(bf16[768,768]{1,0:T(8,128)(2,1)} %param.51) | copy-start | bytes 3538948
  7.2 209.3 %all-gather.25.cloned.1.call-start = ((), (), s32[]{:S(2)}) async-start(), calls=%async_computation.8 | async-start | bytes 1474560 | tf_op jit(solution)/shard_map/all_gather | solution.py:159
  7.9 213.0 %all-gather.23.cloned.1.call-start = ((), (), s32[]{:S(2)}) async-start(), calls=%async_computation.7 | async-start | bytes 1474560 | tf_op jit(solution)/shard_map/all_gather | solution.py:158
  8.7 216.7 %all-gather.21.cloned.1.call-start = ((), (), s32[]{:S(2)}) async-start(), calls=%async_computation.6 | async-start | bytes 1474560 | tf_op jit(solution)/shard_map/all_gather | solution.py:160
  9.4 232.7 %all-gather.27.cloned.1.call-start = ((), (), s32[]{:S(2)}) async-start(), calls=%async_computation.9 | async-start | bytes 1474560 | tf_op jit(solution)/shard_map/all_gather | solution.py:161
  10.0 237.0 %all-gather.29.cloned.1.call-start = ((), (), s32[]{:S(2)}) async-start(), calls=%async_computation.10 | async-start | bytes 5898240 | tf_op jit(solution)/shard_map/all_gather | solution.py:163
  10.6 244.6 %all-gather.31.cloned.1.call-start = ((), (), s32[]{:S(2)}) async-start(), calls=%async_computation.11 | async-start | bytes 5898240 | tf_op jit(solution)/shard_map/all_gather | solution.py:163
  11.2 255.0 %all-gather.33.cloned.1.call-start = ((), (), s32[]{:S(2)}) async-start(), calls=%async_computation.12 | async-start | bytes 1622016 | tf_op jit(solution)/shard_map/all_gather | solution.py:176
  147.2 47.2 %copy-start.61 = (s32[1024]{0:T(1024)S(1)}, s32[1024]{0:T(1024)}, u32[]{:S(2)}) copy-start(s32[1024]{0:T(1024)} %param.30) | copy-start | bytes 12292
  147.2 47.8 %copy-start.2 = (bf16[512,768]{1,0:T(8,128)(2,1)S(1)}, bf16[512,768]{1,0:T(8,128)(2,1)}, u32[]{:S(2)}) copy-start(bf16[512,768]{1,0:T(8,128)(2,1)} %param.27) | copy-start | bytes 2359300
  147.2 48.3 %copy-start.85 = (u32[32]{0:T(128)S(1)}, u32[32]{0:T(128)}, u32[]{:S(2)}) copy-start(u32[32]{0:T(128)} %constant.101) | copy-start | bytes 388
  147.2 48.9 %copy-start.60 = (f32[768]{0:T(1024)S(1)}, f32[768]{0:T(1024)}, u32[]{:S(2)}) copy-start(f32[768]{0:T(1024)} %param.45) | copy-start | bytes 9220
  147.2 60.7 %copy-start.69 = (f32[192]{0:T(256)S(1)}, f32[192]{0:T(256)}, u32[]{:S(2)}) copy-start(f32[192]{0:T(256)} %param.36) | copy-start | bytes 2308
  147.2 61.0 %copy-start.70 = (f32[192]{0:T(256)S(1)}, f32[192]{0:T(256)}, u32[]{:S(2)}) copy-start(f32[192]{0:T(256)} %param.39) | copy-start | bytes 2308
  147.2 69.3 %copy-start.31 = (f32[768]{0:T(1024)S(1)}, f32[768]{0:T(1024)}, u32[]{:S(2)}) copy-start(f32[768]{0:T(1024)} %param.33) | copy-start | bytes 9220
  147.2 69.3 %copy-start.80 = (f32[768]{0:T(1024)S(1)}, f32[768]{0:T(1024)}, u32[]{:S(2)}) copy-start(f32[768]{0:T(1024)} %param.34) | copy-start | bytes 9220
  151.3 253.5 %reduce-scatter.7.cloned.1.call-start = ((), (), s32[]{:S(2)}) async-start(), calls=%async_computation.13 | async-start | bytes 1474560 | tf_op jit(solution)/shard_map/reduce_scatter | solution.py:272
  201.7 53.6 %copy-start.46 = (f32[4,1,768]{2,1,0:T(1,128)}, f32[4,1,768]{2,1,0:T(1,128)S(1)}, u32[]{:S(2)}) copy-start(f32[4,1,768]{2,1,0:T(1,128)S(1)} %all-gather.6) | copy-start | bytes 36868
  268.9 54.8 %copy-start.17 = (f32[32,1024]{1,0:T(8,128)}, f32[32,1024]{1,0:T(8,128)S(1)}, u32[]{:S(2)}) copy-start(f32[32,1024]{1,0:T(8,128)S(1)} %get-tuple-element.72) | copy-start | bytes 393220
  363.9 54.6 %reduce-scatter.9.cloned.1.call-start = ((), (), s32[]{:S(2)}) async-start(), calls=%async_computation.14 | async-start | bytes 1474560 | tf_op jit(solution)/shard_map/reduce_scatter | solution.py:272
  376.2 70.9 %reduce-scatter.11.cloned.1.call-start = ((), (), s32[]{:S(2)}) async-start(), calls=%async_computation.15 | async-start | bytes 1474560 | tf_op jit(solution)/shard_map/reduce_scatter | solution.py:272
  385.0 90.4 %reduce-scatter.13.cloned.1.call-start = ((), (), s32[]{:S(2)}) async-start(), calls=%async_computation.16 | async-start | bytes 1474560 | tf_op jit(solution)/shard_map/reduce_scatter | solution.py:272
  388.1 137.4 %reduce-scatter.15.cloned.1.call-start = ((), (), s32[]{:S(2)}) async-start(), calls=%async_computation.17 | async-start | bytes 5898240 | tf_op jit(solution)/shard_map/reduce_scatter | solution.py:272
  394.8 181.3 %reduce-scatter.17.cloned.1.call-start = ((), (), s32[]{:S(2)}) async-start(), calls=%async_computation.18 | async-start | bytes 5898240 | tf_op jit(solution)/shard_map/reduce_scatter | solution.py:272
  404.8 171.3 %copy-start.51 = (f32[12,64]{1,0:T(8,128)S(1)}, f32[12,64]{1,0:T(8,128)}, u32[]{:S(2)}) copy-start(f32[12,64]{1,0:T(8,128)} %get-tuple-element.79) | copy-start | bytes 9220
  404.8 171.4 %copy-start.28 = (bf16[512,768]{1,0:T(8,128)(2,1)S(1)}, bf16[512,768]{1,0:T(8,128)(2,1)}, u32[]{:S(2)}) copy-start(bf16[512,768]{1,0:T(8,128)(2,1)} %convert_element_type.238) | copy-start | bytes 2359300
  404.8 229.3 %all-gather.35.cloned.1.call-start = ((), (), s32[]{:S(2)}) async-start(), calls=%async_computation.19 | async-start | bytes 2654208 | tf_op jit(solution)/shard_map/all_gather | solution.py:16
  405.4 277.6 %all-gather.37.cloned.1.call-start = ((), (), s32[]{:S(2)}) async-start(), calls=%async_computation.20 | async-start | bytes 2654208 | tf_op jit(solution)/shard_map/all_gather | solution.py:16
  418.5 317.1 %all-gather.39.cloned.1.call-start = ((), (), s32[]{:S(2)}) async-start(), calls=%async_computation.21 | async-start | bytes 2654208 | tf_op jit(solution)/shard_map/all_gather | solution.py:16
  447.1 340.7 %all-gather.41.cloned.1.call-start = ((), (), s32[]{:S(2)}) async-start(), calls=%async_computation.22 | async-start | bytes 2654208 | tf_op jit(solution)/shard_map/all_gather | solution.py:16
  475.3 450.4 %all-gather.43.cloned.1.call-start = ((), (), s32[]{:S(2)}) async-start(), calls=%async_computation.23 | async-start | bytes 10616832 | tf_op jit(solution)/shard_map/all_gather | solution.py:16
  525.6 537.8 %all-gather.45.cloned.1.call-start = ((), (), s32[]{:S(2)}) async-start(), calls=%async_computation.24 | async-start | bytes 10616832 | tf_op jit(solution)/shard_map/all_gather | solution.py:16
  (76 other events, 364.0 us)
Sparse Core Ops, SparseCore 0:
  9.6 20.1 all-gather.24
  31.3 17.4 all-gather.22
  50.4 17.4 all-gather.20
  69.2 17.4 all-gather.26
  88.1 37.4 all-gather.28
  127.0 37.7 all-gather.30
  168.3 55.2 all-gather.32
  364.0 25.6 reduce-scatter.6
  392.8 25.6 reduce-scatter.8
  421.4 25.6 reduce-scatter.10
  449.7 25.6 reduce-scatter.12
  477.7 47.7 reduce-scatter.14
  528.1 47.9 reduce-scatter.16
  578.1 52.2 all-gather.34
  632.4 50.5 all-gather.36
  685.0 50.5 all-gather.38
  737.6 50.1 all-gather.40
  789.9 135.7 all-gather.42
  927.9 135.4 all-gather.44
